TPU v7x, 32 devices: a whole 2x2x4 slice. The times are simulated.
32 devices in a mesh: dp: 8 (over z, y), tp: 4 (over x, core).
Axes of the slice: x: 2, y: 2, z: 4, core: 2. Of those that a mesh axis runs over, the one named last changes fastest.
Arguments:
- tokens: bfloat16 [32, 1024, 768], P(('dp', 'tp')), may hold values from -11 to 11
- clip_lengths: int32 [32, 4], P(('dp', 'tp')), may hold values from 1 to 384, as said below
- out_grad: bfloat16 [32, 1024, 768], P(('dp', 'tp')), may hold values from -6 to 6
- w_query: bfloat16 [768, 768], P(('dp', 'tp')), may hold values from -0.21875 to 0.21875
- w_key: bfloat16 [768, 768], P(('dp', 'tp')), may hold values from -0.21875 to 0.21875
- w_value: bfloat16 [768, 768], P(('dp', 'tp')), may hold values from -0.21875 to 0.21875
- w_output: bfloat16 [768, 768], P(('dp', 'tp')), may hold values from -2.5 to 2.5
- gain_attention: bfloat16 [768], P(('dp', 'tp')), may hold values from 0.099609375 to 1.8984375
- gain_feed: bfloat16 [768], P(('dp', 'tp')), may hold values from 0.099609375 to 1.8984375
- w_expand: bfloat16 [768, 3072], P('dp', 'tp'), may hold values from -0.21875 to 0.21875
- w_reduce: bfloat16 [3072, 768], P('tp', 'dp'), may hold values from -0.4375 to 0.4375
Outputs:
- block_out: bfloat16 [32, 1024, 768], P(('dp', 'tp'))
- grad_tokens: float32 [32, 1024, 768], P(('dp', 'tp'))
- grad_w_query: float32 [768, 768], P(('dp', 'tp'))
- grad_w_key: float32 [768, 768], P(('dp', 'tp'))
- grad_w_value: float32 [768, 768], P(('dp', 'tp'))
- grad_w_output: float32 [768, 768], P(('dp', 'tp'))
- grad_gain_attention: float32 [768], P(('dp', 'tp'))
- grad_gain_feed: float32 [768], P(('dp', 'tp'))
- grad_w_expand: float32 [768, 3072], P('dp', 'tp')
- grad_w_reduce: float32 [3072, 768], P('tp', 'dp')
- root_mean_squares: float32 [3], replicated
Inputs may be any that keep to these rules, and one draw needn't show every extreme that they name: Each row of clip_lengths gives the lengths of its 3 clips in order, each at most 384 with one of exactly 384 in every row, then the number of padding slots at the row's end, 1 to 256; a row's entries sum to 1024.
All inputs are finite; a program needn't handle non-finite values.
Results may differ from a plain program's by a relative error of at most 0.015.
Values may be sent and summed in bfloat16 or wider, within the bound.
A program may use at most 192 MiB of HBM per device.

v0:
```python
from functools import partial
import jax
import jax.numpy as jnp
from jax import lax
from jax.sharding import PartitionSpec as P

HEADS = 12
HEAD_DIM = 64
SLOTS = 4


def segment_numbers(lengths, pack_len):
    clip_ends = jnp.cumsum(lengths[:, :-1], axis=-1, dtype=jnp.int32)
    position = jnp.arange(pack_len, dtype=jnp.int32)
    return jnp.sum(
        (position[None, :, None] >= clip_ends[:, None, :]).astype(jnp.int32),
        axis=-1,
        dtype=jnp.int32,
    )


def normalize(array_in):
    average = jnp.mean(array_in, axis=-1, keepdims=True)
    centred = array_in - average
    spread = jnp.mean(centred * centred, axis=-1, keepdims=True)
    inv_scale = lax.rsqrt(spread + 1e-06)
    return (centred * inv_scale, inv_scale)


def norm_back(grad_normed, unit_value, inv_scale, gain_vec):
    scaled = grad_normed * gain_vec
    inner_sum = (
        scaled
        - jnp.mean(scaled, axis=-1, keepdims=True)
        - unit_value * jnp.mean(scaled * unit_value, axis=-1, keepdims=True)
    )
    return (inv_scale * inner_sum, jnp.sum(grad_normed * unit_value, axis=0))


def dot_plain(left_side, right_side):
    return jnp.dot(left_side, right_side, preferred_element_type=jnp.float32)


def dot_first(left_side, right_side):
    return lax.dot_general(
        left_side, right_side, (((0,), (0,)), ((), ())), preferred_element_type=jnp.float32
    )


def dot_last(left_side, right_side):
    return lax.dot_general(
        left_side, right_side, (((1,), (1,)), ((), ())), preferred_element_type=jnp.float32
    )


def split_heads(array_in, rows_dev, pack_len):
    return (
        array_in.reshape(rows_dev, pack_len, HEADS, HEAD_DIM)
        .transpose(0, 2, 1, 3)
        .reshape(rows_dev * HEADS, pack_len, HEAD_DIM)
    )


def merge_heads(array_in, rows_dev, pack_len):
    return (
        array_in.reshape(rows_dev, HEADS, pack_len, HEAD_DIM)
        .transpose(0, 2, 1, 3)
        .reshape(rows_dev * pack_len, HEADS * HEAD_DIM)
    )


def head_scores(query_head, key_head, segments):
    same_clip = segments[:, None] == segments[None, :]
    scores = dot_last(query_head, key_head) * 0.125
    return jnp.where(same_clip, scores, -1e30)


def head_forward(block_item):
    query_head, key_head, value_head, segments = block_item
    scores = head_scores(query_head, key_head, segments)
    row_max = jnp.max(scores, axis=-1, keepdims=True)
    exponent = jnp.exp(scores - row_max)
    row_sum = jnp.sum(exponent, axis=-1, keepdims=True)
    weights = (exponent / row_sum).astype(jnp.bfloat16)
    return (dot_plain(weights, value_head).astype(jnp.bfloat16), row_max, row_sum)


def head_backward(block_item):
    query_head, key_head, value_head, segments, row_max, row_sum, grad_head = block_item
    scores = head_scores(query_head, key_head, segments)
    probabilities = jnp.exp(scores - row_max) / row_sum
    grad_probs = dot_last(grad_head, value_head)
    grad_value = dot_first(probabilities.astype(jnp.bfloat16), grad_head)
    inner_sum = jnp.sum(probabilities * grad_probs, axis=-1, keepdims=True)
    grad_scores = (probabilities * (grad_probs - inner_sum)).astype(jnp.bfloat16)
    grad_query = (dot_plain(grad_scores, key_head) * 0.125).astype(jnp.bfloat16)
    grad_key = (dot_first(grad_scores, query_head) * 0.125).astype(jnp.bfloat16)
    return (grad_query, grad_key, grad_value.astype(jnp.bfloat16))


def on_device(
    tokens,
    clip_lengths,
    out_grad,
    w_query,
    w_key,
    w_value,
    w_output,
    gain_attention,
    gain_feed,
    w_expand,
    w_reduce,
):
    rows_dev, pack_len, width = tokens.shape
    token_count = rows_dev * pack_len
    segments = segment_numbers(clip_lengths, pack_len)
    valid_rows = (segments < SLOTS - 1).astype(jnp.float32).reshape(-1)
    valid_column = valid_rows[:, None]
    inputs = tokens.reshape(token_count, width).astype(jnp.float32)
    query_full, key_full, value_full, output_full, gain_one, gain_two = (
        lax.all_gather(w_query, ("dp", "tp"), axis=0, tiled=True),
        lax.all_gather(w_key, ("dp", "tp"), axis=0, tiled=True),
        lax.all_gather(w_value, ("dp", "tp"), axis=0, tiled=True),
        lax.all_gather(w_output, ("dp", "tp"), axis=0, tiled=True),
        lax.all_gather(gain_attention, ("dp", "tp"), axis=0, tiled=True),
        lax.all_gather(gain_feed, ("dp", "tp"), axis=0, tiled=True),
    )
    expand_full, reduce_full = (
        lax.all_gather(w_expand, "dp", axis=0, tiled=True),
        lax.all_gather(w_reduce, "dp", axis=1, tiled=True),
    )
    gain_one = gain_one.astype(jnp.float32)
    gain_two = gain_two.astype(jnp.float32)
    unit_one, scale_one = normalize(inputs)
    normed = (unit_one * gain_one).astype(jnp.bfloat16)
    query_rows = dot_plain(normed, query_full).astype(jnp.bfloat16)
    key_rows = dot_plain(normed, key_full).astype(jnp.bfloat16)
    value_rows = dot_plain(normed, value_full).astype(jnp.bfloat16)
    head_segments = jnp.repeat(segments, HEADS, axis=0)
    query_heads = split_heads(query_rows, rows_dev, pack_len)
    key_heads = split_heads(key_rows, rows_dev, pack_len)
    value_heads = split_heads(value_rows, rows_dev, pack_len)
    mixed_heads, row_maxima, row_sums = lax.map(
        head_forward, (query_heads, key_heads, value_heads, head_segments)
    )
    mixed_rows = merge_heads(mixed_heads, rows_dev, pack_len)
    branch = dot_plain(mixed_rows, output_full)
    middle = inputs + branch
    unit_two, scale_two = normalize(middle)
    normed_feed = (unit_two * gain_two).astype(jnp.bfloat16)
    normed_rows = lax.all_gather(normed_feed, "tp", axis=0, tiled=True)
    hidden = dot_plain(normed_rows, expand_full)
    gelu_value, gelu_pull = jax.vjp(partial(jax.nn.gelu, approximate=False), hidden)
    active = gelu_value.astype(jnp.bfloat16)
    feed_out = lax.psum_scatter(
        dot_plain(
            lax.slice_in_dim(active, 0, token_count * lax.axis_size("tp"), axis=0), reduce_full
        ),
        "tp",
        scatter_dimension=0,
        tiled=True,
    )
    result = (middle + feed_out).astype(jnp.bfloat16).reshape(rows_dev, pack_len, width)
    totals_all = lax.psum(
        (
            jnp.sum(inputs * inputs * valid_column),
            jnp.sum(branch * branch * valid_column),
            jnp.sum(feed_out * feed_out * valid_column),
            jnp.sum(valid_rows),
        ),
        ("dp", "tp"),
    )
    rms_stats = jnp.sqrt(jnp.stack(totals_all[:3]) / (totals_all[3] * width))
    grad_result = out_grad.reshape(token_count, width).astype(jnp.float32) * valid_column
    grad_feed = grad_result.astype(jnp.bfloat16)
    grad_rows = lax.all_gather(grad_feed, "tp", axis=0, tiled=True)
    grad_reduce = dot_first(active, grad_rows)
    grad_active = dot_last(grad_rows, reduce_full)
    grad_hidden = gelu_pull(grad_active)[0].astype(jnp.bfloat16)
    grad_expand = dot_first(normed_rows, grad_hidden)
    grad_normed_feed = lax.psum_scatter(
        dot_last(grad_hidden, expand_full), "tp", scatter_dimension=0, tiled=True
    )
    grad_norm_two, grad_gain_two = norm_back(grad_normed_feed, unit_two, scale_two, gain_two)
    grad_middle = grad_result + grad_norm_two
    grad_branch = grad_middle.astype(jnp.bfloat16)
    grad_output_w = dot_first(mixed_rows, grad_branch)
    grad_mixed = dot_last(grad_branch, output_full).astype(jnp.bfloat16)
    grad_heads = split_heads(grad_mixed, rows_dev, pack_len)
    grad_query_heads, grad_key_heads, grad_value_heads = lax.map(
        head_backward,
        (query_heads, key_heads, value_heads, head_segments, row_maxima, row_sums, grad_heads),
    )
    grad_query = merge_heads(grad_query_heads, rows_dev, pack_len)
    grad_key = merge_heads(grad_key_heads, rows_dev, pack_len)
    grad_value = merge_heads(grad_value_heads, rows_dev, pack_len)
    grad_query_w = dot_first(normed, grad_query)
    grad_key_w = dot_first(normed, grad_key)
    grad_value_w = dot_first(normed, grad_value)
    grad_normed = (
        dot_last(grad_query, query_full)
        + dot_last(grad_key, key_full)
        + dot_last(grad_value, value_full)
    )
    grad_norm_one, grad_gain_one = norm_back(grad_normed, unit_one, scale_one, gain_one)
    grad_inputs = (grad_middle + grad_norm_one).reshape(rows_dev, pack_len, width)
    shard_expand, shard_reduce = (
        lax.psum_scatter(grad_expand, "dp", scatter_dimension=0, tiled=True),
        lax.psum_scatter(grad_reduce, "dp", scatter_dimension=1, tiled=True),
    )
    shard_query, shard_key, shard_value, shard_output, shard_gain_one, shard_gain_two = (
        lax.psum_scatter(grad_query_w, ("dp", "tp"), scatter_dimension=0, tiled=True),
        lax.psum_scatter(grad_key_w, ("dp", "tp"), scatter_dimension=0, tiled=True),
        lax.psum_scatter(grad_value_w, ("dp", "tp"), scatter_dimension=0, tiled=True),
        lax.psum_scatter(grad_output_w, ("dp", "tp"), scatter_dimension=0, tiled=True),
        lax.psum_scatter(grad_gain_one, ("dp", "tp"), scatter_dimension=0, tiled=True),
        lax.psum_scatter(grad_gain_two, ("dp", "tp"), scatter_dimension=0, tiled=True),
    )
    return (
        result,
        grad_inputs,
        shard_query,
        shard_key,
        shard_value,
        shard_output,
        shard_gain_one,
        shard_gain_two,
        shard_expand,
        shard_reduce,
        rms_stats,
    )


def solution(mesh):
    in_specs = (
        P(("dp", "tp"), None, None),
        P(("dp", "tp"), None),
        P(("dp", "tp"), None, None),
        P(("dp", "tp"), None),
        P(("dp", "tp"), None),
        P(("dp", "tp"), None),
        P(("dp", "tp"), None),
        P(("dp", "tp")),
        P(("dp", "tp")),
        P("dp", "tp"),
        P("tp", "dp"),
    )
    out_specs = (
        P(("dp", "tp"), None, None),
        P(("dp", "tp"), None, None),
        P(("dp", "tp"), None),
        P(("dp", "tp"), None),
        P(("dp", "tp"), None),
        P(("dp", "tp"), None),
        P(("dp", "tp")),
        P(("dp", "tp")),
        P("dp", "tp"),
        P("tp", "dp"),
        P(),
    )
    return jax.shard_map(
        on_device, mesh=mesh, in_specs=in_specs, out_specs=out_specs, check_vma=False
    )
```

profile of v0, /device:TPU:0, one launch (start us, length us, event | category | flops | bytes accessed | tf_op | source)
XLA Modules:
  0.0 1258.4 jit_solution(7682637012286789652)
XLA Ops:
  13.2 42.1 %all-reduce.5 = (bf16[768]{0:T(1024)(128)(2,1)S(1)}, bf16[768]{0:T(1024)(128)(2,1)S(1)}) all-reduce(bf16[768]{0:T(1024)(128)(2,1)S(1)} %dynamic-update-slice, bf16[768]{0:T(1024)(128)(2,1)S(1)} %dynamic-update-slice.1), channel_id=1, replica_groups=mesh['dp'=8,'tp'=4] {'dp','tp'}, use_global_device_ids=true, to_apply=%add | all-reduce | flops 1536 | bytes 6144
  56.0 11.7 all-gather.9.cloned.1.call-done
  67.8 2.8 convolution_convert_fusion.3
  73.3 50.4 %all-gather.11.cloned.1.call-done = bf16[768,768]{1,0:T(8,128)(2,1)} async-done(((bf16[24,768]{1,0:T(8,128)(2,1)}), bf16[768,768]{1,0:T(8,128)(2,1)}) %all-gather.11.cloned.1.call-update) | async-done | bytes 1179664 | tf_op jit(solution)/shard_map/all_gather | solution.py:122
  123.7 2.8 convolution_convert_fusion.2
  126.5 2.8 copy.44
  129.2 50.3 %all-gather.13.cloned.1.call-done = bf16[768,768]{1,0:T(8,128)(2,1)} async-done(((bf16[24,768]{1,0:T(8,128)(2,1)}), bf16[768,768]{1,0:T(8,128)(2,1)}) %all-gather.13.cloned.1.call-update) | async-done | bytes 1179664 | tf_op jit(solution)/shard_map/all_gather | solution.py:123
  179.6 2.8 convolution_convert_fusion.1
  182.4 2.8 copy.45
  185.4 68.7 %while.28 = (s32[]{:T(128)}, bf16[12,1024,64]{1,2,0:T(8,128)(2,1)S(1)}, f32[12,1024,1]{1,2,0:T(1,128)}, f32[12,1024,1]{1,2,0:T(1,128)}, s32[12,1024]{1,0:T(8,128...) while((s32[]{:T(128)}, ...), condition=%wide.region_7.8_spmd, body=%wide.region_4.7_spmd.sunk | while | flops 284227584 | bytes 13568109 | solution.py:143
  254.2 5.0 fusion.102
  265.7 11.7 all-gather.19.cloned.1.call-done
  277.4 47.2 %all-gather.17.cloned.1.call-done = bf16[4096,768]{0,1:T(8,128)(2,1)} async-done(((bf16[1024,768]{0,1:T(8,128)(2,1)}), bf16[4096,768]{0,1:T(8,128)(2,1)}) %all-gather.17.cloned.1.call-update) | async-done | bytes 6291472 | tf_op jit(solution)/shard_map/all_gather | solution.py:151
  324.5 10.2 fusion.104
  334.7 33.1 %all-gather.21.cloned.1.call-done = bf16[768,768]{0,1:T(8,128)(2,1)} async-done(((bf16[768,96]{0,1:T(8,128)(2,1)}), bf16[768,768]{0,1:T(8,128)(2,1)}) %all-gather.21.cloned.1.call-update) | async-done | bytes 1179664 | tf_op jit(solution)/shard_map/all_gather | solution.py:130
  367.8 46.7 %all-gather.23.cloned.1.call-done = bf16[4096,768]{0,1:T(8,128)(2,1)} async-done(((bf16[1024,768]{0,1:T(8,128)(2,1)}), bf16[4096,768]{0,1:T(8,128)(2,1)}) %all-gather.23.cloned.1.call-update) | async-done | bytes 6291472 | tf_op jit(solution)/shard_map/all_gather | solution.py:176
  414.6 36.4 %add_convert_fusion = (bf16[4096,768]{1,0:T(8,128)(2,1)S(1)}, f32[4096,768]{1,0:T(8,128)}) fusion(f32[4096,768]{1,0:T(8,128)} %fusion.104, bf16[4096,768]{0,1:T(8,128)(2,1)} %all-gather.23.cloned.1.call-done, bf16[768,768]{0,1:T(8,128)(2,1)} %all-gather.21.cloned.1.call-done), kind=kOutput, calls=%fused_computation.64 | convolution fusion | flops 5058330624 | bytes 38928384 | tf_op jit(solution)/shard_map/dot_general | solution.py:51
  453.5 8.0 fusion.106
  461.6 11.3 multiply_convert_fusion.1
  472.9 3.7 copy-done.10
  476.6 7.9 fusion.105
  484.6 10.4 fusion.107
  495.1 10.1 fusion.110
  505.3 55.4 %reduce-scatter.11.cloned.1.call-done = f32[1024,768]{0,1:T(8,128)} async-done(((f32[4096,768]{0,1:T(8,128)}), f32[1024,768]{0,1:T(8,128)}) %reduce-scatter.11.cloned.1.call-update) | async-done | bytes 3145744 | tf_op jit(solution)/shard_map/reduce_scatter | solution.py:181
  560.7 2.9 multiply_reduce_fusion.3
  563.6 98.6 %reduce-scatter.9.cloned.1.call-done = f32[1024,768]{0,1:T(8,128)} async-done(((f32[4096,768]{0,1:T(8,128)}), f32[1024,768]{0,1:T(8,128)}) %reduce-scatter.9.cloned.1.call-update) | async-done | bytes 3145744 | tf_op jit(solution)/shard_map/reduce_scatter | solution.py:155
  662.3 6.7 multiply_reduce_fusion.2
  670.6 2.8 copy.49
  676.3 160.4 %while.29 = (s32[]{:T(128)}, bf16[12,1024,64]{1,2,0:T(8,128)(2,1)S(1)}, bf16[12,1024,64]{1,2,0:T(8,128)(2,1)}, bf16[12,1024,64]{1,2,0:T(8,128)(2,1)}, s32[12,102...) while((s32[]{:T(128)}, ...), condition=%wide.region_16.17_spmd, body=%wide.region_14.16_spmd.sunk | while | flops 682949632 | bytes 33739908 | solution.py:190
  679.6 2.7 multiply_reduce_fusion.9
  693.0 2.7 multiply_reduce_fusion.9
  719.7 2.8 multiply_reduce_fusion.9
  746.4 2.7 multiply_reduce_fusion.9
  759.8 2.7 multiply_reduce_fusion.9
  786.5 2.7 multiply_reduce_fusion.9
  826.6 2.7 multiply_reduce_fusion.9
  836.7 2.9 fusion.96
  839.7 4.3 fusion.94
  844.0 4.5 fusion.92
  848.6 4.8 fusion.86
  856.6 3.3 fusion.108
  861.7 2.9 fusion.75
  867.3 3.6 copy.51
  870.8 39.8 %all-reduce.4 = (f32[768]{0:T(1024)S(1)}, f32[768]{0:T(1024)S(1)}, f32[1]{0:T(128)}, f32[1]{0:T(128)}, f32[1]{0:T(128)}, /*index=5*/f32[]{:T(128)}) all-reduce(f32[768]{0:T(1024)S(1)} %get-tuple-element.155, f32[768]{0:T(1024)S(1)} %get-tuple-element.153, f32[1]{0:T(128)} %bitcast.60, ...), channel_id=8, replica_groups=mesh['dp'=8,'tp'=4] {'dp','tp'}, use_global_device_ids=true, to_apply=%region_24.25.clone | all-reduce | flops 1540 | bytes 12320
  914.8 23.9 %reduce-scatter.13.cloned.1.call-done = f32[24,768]{1,0:T(8,128)} async-done(((f32[768,768]{1,0:T(8,128)}), f32[24,768]{1,0:T(8,128)}) %reduce-scatter.13.cloned.1.call-update) | async-done | bytes 73744 | tf_op jit(solution)/shard_map/reduce_scatter | solution.py:212
  938.7 104.6 %reduce-scatter.15.cloned.1.call-done = f32[24,768]{1,0:T(8,128)} async-done(((f32[768,768]{1,0:T(8,128)}), f32[24,768]{1,0:T(8,128)}) %reduce-scatter.15.cloned.1.call-update) | async-done | bytes 73744 | tf_op jit(solution)/shard_map/reduce_scatter | solution.py:213
  1043.3 103.7 %reduce-scatter.17.cloned.1.call-done = f32[24,768]{1,0:T(8,128)} async-done(((f32[768,768]{1,0:T(8,128)}), f32[24,768]{1,0:T(8,128)}) %reduce-scatter.17.cloned.1.call-update) | async-done | bytes 73744 | tf_op jit(solution)/shard_map/reduce_scatter | solution.py:214
  1147.0 104.7 %reduce-scatter.19.cloned.1.call-done = f32[24,768]{1,0:T(8,128)} async-done(((f32[768,768]{1,0:T(8,128)}), f32[24,768]{1,0:T(8,128)}) %reduce-scatter.19.cloned.1.call-update) | async-done | bytes 73744 | tf_op jit(solution)/shard_map/reduce_scatter | solution.py:215
  (304 shorter events, 244.1 us)
Async XLA Ops:
  7.2 5.2 copy-start.37
  7.2 5.5 copy-start.38
  7.2 5.8 copy-start.39
  7.2 60.6 %all-gather.9.cloned.1.call-start = ((), (), s32[]{:S(2)}) async-start(), calls=%async_computation.8 | async-start | bytes 1216512 | tf_op jit(solution)/shard_map/all_gather | solution.py:121
  7.9 115.7 %all-gather.11.cloned.1.call-start = ((), (), s32[]{:S(2)}) async-start(), calls=%async_computation.9 | async-start | bytes 1216512 | tf_op jit(solution)/shard_map/all_gather | solution.py:122
  8.7 170.9 %all-gather.13.cloned.1.call-start = ((), (), s32[]{:S(2)}) async-start(), calls=%async_computation.10 | async-start | bytes 1216512 | tf_op jit(solution)/shard_map/all_gather | solution.py:123
  9.4 244.7 %all-gather.15.cloned.1.call-start = ((), (), s32[]{:S(2)}) async-start(), calls=%async_computation.11 | async-start | bytes 1216512 | tf_op jit(solution)/shard_map/all_gather | solution.py:124
  10.0 267.4 %all-gather.19.cloned.1.call-start = ((), (), s32[]{:S(2)}) async-start(), calls=%async_computation.13 | async-start | bytes 1327104 | tf_op jit(solution)/shard_map/all_gather | solution.py:129
  10.6 314.0 %all-gather.17.cloned.1.call-start = ((), (), s32[]{:S(2)}) async-start(), calls=%async_computation.12 | async-start | bytes 7864320 | tf_op jit(solution)/shard_map/all_gather | solution.py:151
  12.4 241.8 %copy-start.2 = (bf16[1,1024,768]{1,2,0:T(8,128)(2,1)}, bf16[1,1024,768]{1,2,0:T(8,128)(2,1)S(1)}, u32[]{:S(2)}) copy-start(bf16[1,1024,768]{1,2,0:T(8,128)(2,1)S(1)} %copy.42) | copy-start | bytes 4718596
  12.7 251.3 %copy-start.19 = (s32[1024]{0:T(1024)}, s32[1024]{0:T(1024)S(1)}, u32[]{:S(2)}) copy-start(s32[1024]{0:T(1024)S(1)} %fusion.89) | copy-start | bytes 12292
  55.2 124.3 %copy-start.29 = (f32[768]{0:T(1024)}, f32[768]{0:T(1024)S(1)}, u32[]{:S(2)}) copy-start(f32[768]{0:T(1024)S(1)} %convert_element_type.106) | copy-start | bytes 9220
  55.5 124.0 %copy-start.25 = (f32[1024]{0:T(1024)}, f32[1024]{0:T(1024)S(1)}, u32[]{:S(2)}) copy-start(f32[1024]{0:T(1024)S(1)} %broadcast_multiply_fusion.5) | copy-start | bytes 12292
  56.0 123.6 %copy-start.31 = (f32[1024]{0:T(1024)}, f32[1024]{0:T(1024)S(1)}, u32[]{:S(2)}) copy-start(f32[1024]{0:T(1024)S(1)} %add_rsqrt_fusion.1) | copy-start | bytes 12292
  56.0 203.5 %copy-start.21 = (f32[768]{0:T(1024)}, f32[768]{0:T(1024)S(1)}, u32[]{:S(2)}) copy-start(f32[768]{0:T(1024)S(1)} %convert_element_type.111) | copy-start | bytes 9220
  254.1 5.0 copy-start.7
  254.1 5.0 copy-start.16
  262.4 105.5 %all-gather.21.cloned.1.call-start = ((), (), s32[]{:S(2)}) async-start(), calls=%async_computation.14 | async-start | bytes 1327104 | tf_op jit(solution)/shard_map/all_gather | solution.py:130
  263.1 151.4 %all-gather.23.cloned.1.call-start = ((), (), s32[]{:S(2)}) async-start(), calls=%async_computation.16 | async-start | bytes 7864320 | tf_op jit(solution)/shard_map/all_gather | solution.py:176
  263.9 70.8 %copy-start.4 = (bf16[1,1024,768]{1,2,0:T(8,128)(2,1)}, bf16[1,1024,768]{1,2,0:T(8,128)(2,1)S(1)}, u32[]{:S(2)}) copy-start(bf16[1,1024,768]{1,2,0:T(8,128)(2,1)S(1)} %copy.47) | copy-start | bytes 4718596
  264.0 70.8 %copy-start.27 = (f32[1024]{0:T(1024)}, f32[1024]{0:T(1024)S(1)}, u32[]{:S(2)}) copy-start(f32[1024]{0:T(1024)S(1)} %compare_convert_fusion.1) | copy-start | bytes 12292
  265.6 295.1 %reduce-scatter.11.cloned.1.call-start = ((), (), s32[]{:S(2)}) async-start(), calls=%async_computation.17 | async-start | bytes 15728640 | tf_op jit(solution)/shard_map/reduce_scatter | solution.py:181
  334.7 118.8 %copy-start.35 = (bf16[768,768]{1,0:T(8,128)(2,1)S(1)}, bf16[768,768]{1,0:T(8,128)(2,1)}, u32[]{:S(2)}) copy-start(bf16[768,768]{1,0:T(8,128)(2,1)} %all-gather.19.cloned.1.call-done) | copy-start | bytes 3538948
  461.5 200.7 %reduce-scatter.9.cloned.1.call-start = ((), (), s32[]{:S(2)}) async-start(), calls=%async_computation.15 | async-start | bytes 15728640 | tf_op jit(solution)/shard_map/reduce_scatter | solution.py:155
  461.6 15.1 %copy-start.36 = (bf16[768,768]{0,1:T(8,128)(2,1)S(1)}, bf16[768,768]{0,1:T(8,128)(2,1)}, u32[]{:S(2)}) copy-start(bf16[768,768]{0,1:T(8,128)(2,1)} %all-gather.21.cloned.1.call-done) | copy-start | bytes 3538948
  472.9 3.8 copy-start.10
  484.6 430.2 %reduce-scatter.21.cloned.1.call-start = ((), (), s32[]{:S(2)}) async-start(), calls=%async_computation.22 | async-start | bytes 2654208 | tf_op jit(solution)/shard_map/reduce_scatter | solution.py:208
  495.1 65.7 %copy-start.18 = (f32[1024]{0:T(1024)S(1)}, f32[1024]{0:T(1024)}, u32[]{:S(2)}) copy-start(f32[1024]{0:T(1024)} %copy-done.17) | copy-start | bytes 12292
  495.1 65.7 %copy-start.22 = (f32[768]{0:T(1024)S(1)}, f32[768]{0:T(1024)}, u32[]{:S(2)}) copy-start(f32[768]{0:T(1024)} %copy-done.21) | copy-start | bytes 9220
  495.1 65.7 %copy-start.24 = (f32[1024]{0:T(1024)S(1)}, f32[1024]{0:T(1024)}, u32[]{:S(2)}) copy-start(f32[1024]{0:T(1024)} %copy-done.23) | copy-start | bytes 12292
  495.1 419.7 %reduce-scatter.23.cloned.1.call-start = ((), (), s32[]{:S(2)}) async-start(), calls=%async_computation.23 | async-start | bytes 2654208 | tf_op jit(solution)/shard_map/reduce_scatter | solution.py:209
  495.1 65.6 %copy-start.1 = (f32[1024,768]{0,1:T(8,128)S(1)}, f32[1024,768]{0,1:T(8,128)}, u32[]{:S(2)}) copy-start(f32[1024,768]{0,1:T(8,128)} %copy-done) | copy-start | bytes 9437188
  505.3 157.0 %copy-start.28 = (f32[1024]{0:T(1024)S(1)}, f32[1024]{0:T(1024)}, u32[]{:S(2)}) copy-start(f32[1024]{0:T(1024)} %copy-done.27) | copy-start | bytes 12292
  505.3 433.4 %reduce-scatter.13.cloned.1.call-start = ((), (), s32[]{:S(2)}) async-start(), calls=%async_computation.18 | async-start | bytes 2433024 | tf_op jit(solution)/shard_map/reduce_scatter | solution.py:212
  662.3 6.7 copy-start.15
  676.3 160.4 %copy-start.3 = (bf16[1,1024,768]{1,2,0:T(8,128)(2,1)S(1)}, bf16[1,1024,768]{1,2,0:T(8,128)(2,1)}, u32[]{:S(2)}) copy-start(bf16[1,1024,768]{1,2,0:T(8,128)(2,1)} %copy-done.2) | copy-start | bytes 4718596
  676.3 160.4 %copy-start.26 = (f32[1024]{0:T(1024)S(1)}, f32[1024]{0:T(1024)}, u32[]{:S(2)}) copy-start(f32[1024]{0:T(1024)} %copy-done.25) | copy-start | bytes 12292
  676.3 160.4 %copy-start.30 = (f32[768]{0:T(1024)S(1)}, f32[768]{0:T(1024)}, u32[]{:S(2)}) copy-start(f32[768]{0:T(1024)} %copy-done.29) | copy-start | bytes 9220
  676.3 160.4 %copy-start.32 = (f32[1024]{0:T(1024)S(1)}, f32[1024]{0:T(1024)}, u32[]{:S(2)}) copy-start(f32[1024]{0:T(1024)} %copy-done.31) | copy-start | bytes 12292
  836.7 2.9 copy-start.12
  839.6 203.7 %reduce-scatter.15.cloned.1.call-start = ((), (), s32[]{:S(2)}) async-start(), calls=%async_computation.19 | async-start | bytes 2433024 | tf_op jit(solution)/shard_map/reduce_scatter | solution.py:213
  844.0 303.0 %reduce-scatter.17.cloned.1.call-start = ((), (), s32[]{:S(2)}) async-start(), calls=%async_computation.20 | async-start | bytes 2433024 | tf_op jit(solution)/shard_map/reduce_scatter | solution.py:214
  844.0 4.6 copy-start.8
  848.6 4.9 copy-start.20
  848.6 403.1 %reduce-scatter.19.cloned.1.call-start = ((), (), s32[]{:S(2)}) async-start(), calls=%async_computation.21 | async-start | bytes 2433024 | tf_op jit(solution)/shard_map/reduce_scatter | solution.py:215
  856.6 3.3 copy-start.13
  856.6 3.3 copy-start.33
  861.7 2.9 copy-start.6
  (9 other events, 16.1 us)
Sparse Core Ops, SparseCore 0:
  10.9 56.7 all-gather.8
  70.7 52.9 all-gather.10
  126.6 52.9 all-gather.12
  182.3 52.9 all-gather.14
  237.4 39.9 all-gather.18
  279.4 45.1 all-gather.16
  326.7 41.0 all-gather.20
  369.4 45.1 all-gather.22
  461.6 99.0 reduce-scatter.10
  563.2 99.0 reduce-scatter.8
  666.3 68.9 reduce-scatter.20
  739.3 68.2 reduce-scatter.22
  839.7 98.9 reduce-scatter.12
  945.3 97.9 reduce-scatter.14
  1049.1 97.9 reduce-scatter.16
  1153.6 98.0 reduce-scatter.18
where the time goes:
time: 1270 us; the launch traced here: 1260 us
  waiting for transfers between devices  746 us (59%)
  matrix products  299 us (24%)
  blocking collectives  81.8 us (6%)
  local copies, waits for them, and re-layouts  57.7 us (5%)
  other arithmetic  57.1 us (4%)
  between operations  15.3 us (1%)
    dot_general x42, matrix products, dot_last(): lax.dot_general(left_side, right_side, (((1,), (1,)), ((), ())), preferre...  128 us
    reduce_scatter x1, waiting for transfers between devices, on_device(): lax.psum_scatter(grad_output_w, ('dp', 'tp'), scatter_dimension=0, tiled=...  105 us
    reduce_scatter x1, waiting for transfers between devices, on_device(): lax.psum_scatter(grad_key_w, ('dp', 'tp'), scatter_dimension=0, tiled=True)  105 us
    reduce_scatter x1, waiting for transfers between devices, on_device(): lax.psum_scatter(grad_value_w, ('dp', 'tp'), scatter_dimension=0, tiled=T...  104 us
    reduce_scatter x1, waiting for transfers between devices, on_device(): lax.psum_scatter(dot_plain(lax.slice_in_dim(active, 0, token_count * lax....  98.6 us
    dot_general x30, matrix products, dot_first(): lax.dot_general(left_side, right_side, (((0,), (0,)), ((), ())), preferre...  94.1 us
    unnamed x2, blocking collectives  81.8 us
    dot_general x30, matrix products, dot_plain(): return jnp.dot(left_side, right_side, preferred_element_type=jnp.float32)  76.9 us
  transfers between devices with their start and end apart: 16, of which 13 were waited for; matrix products, arithmetic and copies ran while one was open for 29% of the time, Pallas kernels for 0%

commit v1 on v0

--- a/solution.py
+++ b/solution.py
@@ -173,7 +173,12 @@
     rms_stats = jnp.sqrt(jnp.stack(totals_all[:3]) / (totals_all[3] * width))
     grad_result = out_grad.reshape(token_count, width).astype(jnp.float32) * valid_column
     grad_feed = grad_result.astype(jnp.bfloat16)
-    grad_rows = lax.all_gather(grad_feed, "tp", axis=0, tiled=True)
+    ring = [grad_feed]
+    for hop in range(3):
+        ring.append(lax.ppermute(ring[-1], "tp", [(dev, (dev + 1) % 4) for dev in range(4)]))
+    grad_rows = jnp.roll(
+        jnp.concatenate(ring[::-1], axis=0), (lax.axis_index("tp") + 1) * ring[0].shape[0], axis=0
+    )
     grad_reduce = dot_first(active, grad_rows)
     grad_active = dot_last(grad_rows, reduce_full)
     grad_hidden = gelu_pull(grad_active)[0].astype(jnp.bfloat16)

time: 1270 us -> 1220 us (0.961)
  waiting for transfers between devices: 746 us -> 664 us
  matrix products: 299 us -> 314 us
  local copies, waits for them, and re-layouts: 57.7 us -> 71.4 us
    reduce_scatter x1, waiting for transfers between devices: 105 us -> 0.01 us  [on_device(): lax.psum_scatter(grad_output_w, ('dp', 'tp'), scatter_dimension=0, tiled=...]
    ppermute x0 -> x3, waiting for transfers between devices: none -> 87.5 us  [on_device(): lax.ppermute(ring[-1], 'tp', [(dev, (dev + 1) % 4) for dev in range(4)])]
    reduce_scatter x1, waiting for transfers between devices: 23.9 us -> 94.3 us  [on_device(): lax.psum_scatter(grad_query_w, ('dp', 'tp'), scatter_dimension=0, tiled=T...]
    all_gather x1, waiting for transfers between devices: 47.2 us -> 0.01 us  [on_device(): normed_rows = lax.all_gather(normed_feed, 'tp', axis=0, tiled=True)]
    all_gather x1 -> x0, waiting for transfers between devices: 46.7 us -> none  [on_device(): grad_rows = lax.all_gather(grad_feed, 'tp', axis=0, tiled=True)]
    all_gather x1, waiting for transfers between devices: 50.3 us -> 9.91 us  [on_device(): lax.all_gather(w_value, ('dp', 'tp'), axis=0, tiled=True)]
    all_gather x1, waiting for transfers between devices: 11.7 us -> 50.3 us  [on_device(): lax.all_gather(w_query, ('dp', 'tp'), axis=0, tiled=True)]
    dot_general x30, matrix products: 76.9 us -> 114 us  [dot_plain(): return jnp.dot(left_side, right_side, preferred_element_type=jnp.float32)]
  transfers between devices with their start and end apart: 16 -> 18, of which waited for: 13 -> 11; matrix products, arithmetic and copies ran while one was open for 29% -> 34% of each run, Pallas kernels for 0% -> 0%
where the time goes in v1:
time: 1220 us; the launch traced here: 1200 us
  waiting for transfers between devices  664 us (54%)
  matrix products  314 us (26%)
  blocking collectives  81.8 us (7%)
  local copies, waits for them, and re-layouts  71.4 us (6%)
  other arithmetic  51.4 us (4%)
  between operations  15.5 us (1%)
    dot_general x30, matrix products, dot_plain(): return jnp.dot(left_side, right_side, preferred_element_type=jnp.float32)  114 us
    dot_general x42, matrix products, dot_last(): lax.dot_general(left_side, right_side, (((1,), (1,)), ((), ())), preferre...  112 us
    reduce_scatter x1, waiting for transfers between devices, on_device(): lax.psum_scatter(grad_value_w, ('dp', 'tp'), scatter_dimension=0, tiled=T...  105 us
    reduce_scatter x1, waiting for transfers between devices, on_device(): lax.psum_scatter(grad_key_w, ('dp', 'tp'), scatter_dimension=0, tiled=True)  104 us
    reduce_scatter x1, waiting for transfers between devices, on_device(): lax.psum_scatter(dot_plain(lax.slice_in_dim(active, 0, token_count * lax....  98.8 us
    reduce_scatter x1, waiting for transfers between devices, on_device(): lax.psum_scatter(grad_query_w, ('dp', 'tp'), scatter_dimension=0, tiled=T...  94.3 us
    dot_general x30, matrix products, dot_first(): lax.dot_general(left_side, right_side, (((0,), (0,)), ((), ())), preferre...  88.2 us
    ppermute x3, waiting for transfers between devices, on_device(): lax.ppermute(ring[-1], 'tp', [(dev, (dev + 1) % 4) for dev in range(4)])  87.5 us
  transfers between devices with their start and end apart: 18, of which 11 were waited for; matrix products, arithmetic and copies ran while one was open for 34% of the time, Pallas kernels for 0%

profile of v1, /device:TPU:0, one launch (start us, length us, event | category | flops | bytes accessed | tf_op | source)
XLA Modules:
  0.0 1202.6 jit_solution(17534641357590016185)
XLA Ops:
  13.1 42.1 %all-reduce.5 = (bf16[768]{0:T(1024)(128)(2,1)S(1)}, bf16[768]{0:T(1024)(128)(2,1)S(1)}) all-reduce(bf16[768]{0:T(1024)(128)(2,1)S(1)} %dynamic-update-slice, bf16[768]{0:T(1024)(128)(2,1)S(1)} %dynamic-update-slice.1), channel_id=1, replica_groups=mesh['dp'=8,'tp'=4] {'dp','tp'}, use_global_device_ids=true, to_apply=%add | all-reduce | flops 1536 | bytes 6144
  57.8 9.9 all-gather.12.cloned.1.call-done
  67.7 2.8 convolution_convert_fusion.1
  70.5 2.8 copy.45
  73.3 50.3 %all-gather.10.cloned.1.call-done = bf16[768,768]{1,0:T(8,128)(2,1)} async-done(((bf16[24,768]{1,0:T(8,128)(2,1)}), bf16[768,768]{1,0:T(8,128)(2,1)}) %all-gather.10.cloned.1.call-update) | async-done | bytes 1179664 | tf_op jit(solution)/shard_map/all_gather | solution.py:122
  123.6 2.8 convolution_convert_fusion.2
  126.4 2.8 copy.44
  129.2 50.3 %all-gather.8.cloned.1.call-done = bf16[768,768]{1,0:T(8,128)(2,1)} async-done(((bf16[24,768]{1,0:T(8,128)(2,1)}), bf16[768,768]{1,0:T(8,128)(2,1)}) %all-gather.8.cloned.1.call-update) | async-done | bytes 1179664 | tf_op jit(solution)/shard_map/all_gather | solution.py:121
  179.5 2.8 convolution_convert_fusion.3
  185.3 68.9 %while.28 = (s32[]{:T(128)}, bf16[12,1024,64]{1,2,0:T(8,128)(2,1)S(1)}, f32[12,1024,1]{1,2,0:T(1,128)}, f32[12,1024,1]{1,2,0:T(1,128)}, s32[12,1024]{1,0:T(8,128...) while((s32[]{:T(128)}, ...), condition=%wide.region_7.8_spmd, body=%wide.region_4.7_spmd.sunk | while | flops 284227584 | bytes 13568109 | solution.py:143
  254.3 5.0 fusion.110
  264.1 19.5 %collective-permute-done = bf16[1024,768]{0,1:T(8,128)(2,1)S(1)} collective-permute-done((bf16[1024,768]{0,1:T(8,128)(2,1)S(1)}, bf16[1024,768]{0,1:T(8,128)(2,1)S(1)}, u32[]{:S(2)}, u32[]{:S(2)}) %collective-permute-start) | collective-permute-done | bytes 1572896 | tf_op jit(solution)/shard_map/ppermute | solution.py:178
  283.7 48.6 %collective-permute-done.1 = bf16[1024,768]{0,1:T(8,128)(2,1)} collective-permute-done((bf16[1024,768]{0,1:T(8,128)(2,1)S(1)}, bf16[1024,768]{0,1:T(8,128)(2,1)}, u32[]{:S(2)}, u32[]{:S(2)}) %collective-permute-start.1) | collective-permute-done | bytes 1572896 | tf_op jit(solution)/shard_map/ppermute | solution.py:178
  334.9 19.3 %collective-permute-done.2 = bf16[1024,768]{0,1:T(8,128)(2,1)} collective-permute-done((bf16[1024,768]{0,1:T(8,128)(2,1)}, bf16[1024,768]{0,1:T(8,128)(2,1)}, u32[]{:S(2)}, u32[]{:S(2)}) %collective-permute-start.2) | collective-permute-done | bytes 1572896 | tf_op jit(solution)/shard_map/ppermute | solution.py:178
  354.2 2.8 constant_dynamic-update-slice_fusion.9
  357.0 2.8 constant_dynamic-update-slice_fusion.8
  362.7 2.8 constant_dynamic-update-slice_fusion.5
  365.6 2.9 constant_dynamic-update-slice_fusion.4
  371.4 34.8 %multiply_convert_fusion.1 = (bf16[4096,768]{1,0:T(8,128)(2,1)}, f32[4096,768]{1,0:T(8,128)}, f32[4096,768]{1,0:T(8,128)}) fusion(bf16[4096,768]{0,1:T(8,128)(2,1)} %all-gather.16.cloned.1.call-done, bf16[768,768]{1,0:T(8,128)(2,1)} %all-gather.18.cloned.1.call-done), kind=kOutput, calls=%fused_computation.65 | convolution fusion | flops 5036310528 | bytes 38928384 | tf_op jit(solution)/shard_map/dot_general | solution.py:41
  406.2 16.9 %add_convert_fusion = bf16[4096,768]{1,0:T(8,128)(2,1)S(1)} fusion(f32[4096,768]{1,0:T(8,128)} %get-tuple-element.209, f32[4096,768]{1,0:T(8,128)} %get-tuple-element.223, bf16[768,768]{0,1:T(8,128)(2,1)} %all-gather.20.cloned.1.call-done, bf16[8192,768]{0,1:T(8,128)(2,1)} %constant_dynamic-update-slice_fusion.2, s32[]{:T(128)S(6)} %select_n.21), kind=kOutput, calls=%fused_computation.64 | convolution fusion | flops 4875878400 | bytes 38928388 | tf_op jit(solution)/shard_map/dot_general | solution.py:51
  425.7 7.9 fusion.113
  434.9 12.9 %fusion.112 = f32[4096,768]{0,1:T(8,128)} fusion(bf16[4096,768]{1,0:T(8,128)(2,1)} %get-tuple-element.208, bf16[768,768]{0,1:T(8,128)(2,1)S(1)} %copy-done.34), kind=kOutput, calls=%fused_computation.159 | convolution fusion | flops 4831838208 | bytes 20054016 | tf_op jit(solution)/shard_map/dot_general | solution.py:41
  447.8 11.3 fusion.114
  459.3 11.2 fusion.60
  470.5 61.2 %reduce-scatter.11.cloned.1.call-done = f32[1024,768]{0,1:T(8,128)} async-done(((f32[4096,768]{0,1:T(8,128)}), f32[1024,768]{0,1:T(8,128)}) %reduce-scatter.11.cloned.1.call-update) | async-done | bytes 3145744 | tf_op jit(solution)/shard_map/reduce_scatter | solution.py:186
  531.8 2.9 multiply_reduce_fusion.3
  534.7 98.8 %reduce-scatter.9.cloned.1.call-done = f32[1024,768]{0,1:T(8,128)} async-done(((f32[4096,768]{0,1:T(8,128)}), f32[1024,768]{0,1:T(8,128)}) %reduce-scatter.9.cloned.1.call-update) | async-done | bytes 3145744 | tf_op jit(solution)/shard_map/reduce_scatter | solution.py:155
  633.5 6.7 multiply_reduce_fusion.2
  642.7 4.3 copy.49
  647.0 4.3 fusion.92
  654.3 160.6 %while.29 = (s32[]{:T(128)}, bf16[12,1024,64]{1,2,0:T(8,128)(2,1)}, bf16[12,1024,64]{1,2,0:T(8,128)(2,1)}, bf16[12,1024,64]{1,2,0:T(8,128)(2,1)S(1)}, s32[12,102...) while((s32[]{:T(128)}, bf16[12,1024,64]{1,2,0:T(8,128)(2,1)}, ...), condition=%wide.region_16.17_spmd, body=%wide.region_14.16_spmd.sunk | while | flops 682949632 | bytes 33739908 | solution.py:195
  657.8 2.7 multiply_reduce_fusion.9
  671.2 2.7 multiply_reduce_fusion.9
  684.6 2.7 multiply_reduce_fusion.9
  697.9 2.7 multiply_reduce_fusion.9
  751.3 2.7 multiply_reduce_fusion.9
  764.7 2.7 multiply_reduce_fusion.9
  814.9 4.9 fusion.104
  819.9 4.4 fusion.102
  824.3 2.9 fusion.100
  830.2 3.6 fusion.115
  835.6 4.3 fusion.79
  839.9 39.7 %all-reduce.4 = (f32[768]{0:T(1024)S(1)}, f32[768]{0:T(1024)S(1)}, f32[1]{0:T(128)}, f32[1]{0:T(128)}, f32[1]{0:T(128)}, /*index=5*/f32[]{:T(128)}) all-reduce(f32[768]{0:T(1024)S(1)} %get-tuple-element.155, f32[768]{0:T(1024)S(1)} %get-tuple-element.153, f32[1]{0:T(128)} %bitcast.60, ...), channel_id=8, replica_groups=mesh['dp'=8,'tp'=4] {'dp','tp'}, use_global_device_ids=true, to_apply=%region_24.25.clone | all-reduce | flops 1540 | bytes 12320
  880.8 5.5 fusion.78
  886.3 3.5 copy.51
  893.0 94.3 %reduce-scatter.13.cloned.1.call-done = f32[24,768]{1,0:T(8,128)} async-done(((f32[768,768]{1,0:T(8,128)}), f32[24,768]{1,0:T(8,128)}) %reduce-scatter.13.cloned.1.call-update) | async-done | bytes 73744 | tf_op jit(solution)/shard_map/reduce_scatter | solution.py:217
  987.3 103.8 %reduce-scatter.15.cloned.1.call-done = f32[24,768]{1,0:T(8,128)} async-done(((f32[768,768]{1,0:T(8,128)}), f32[24,768]{1,0:T(8,128)}) %reduce-scatter.15.cloned.1.call-update) | async-done | bytes 73744 | tf_op jit(solution)/shard_map/reduce_scatter | solution.py:218
  1091.1 104.6 %reduce-scatter.17.cloned.1.call-done = f32[24,768]{1,0:T(8,128)} async-done(((f32[768,768]{1,0:T(8,128)}), f32[24,768]{1,0:T(8,128)}) %reduce-scatter.17.cloned.1.call-update) | async-done | bytes 73744 | tf_op jit(solution)/shard_map/reduce_scatter | solution.py:219
  (304 shorter events, 254.7 us)
Async XLA Ops:
  7.2 60.6 %all-gather.12.cloned.1.call-start = ((), (), s32[]{:S(2)}) async-start(), calls=%async_computation.10 | async-start | bytes 1216512 | tf_op jit(solution)/shard_map/all_gather | solution.py:123
  7.9 115.7 %all-gather.10.cloned.1.call-start = ((), (), s32[]{:S(2)}) async-start(), calls=%async_computation.9 | async-start | bytes 1216512 | tf_op jit(solution)/shard_map/all_gather | solution.py:122
  8.7 170.9 %all-gather.8.cloned.1.call-start = ((), (), s32[]{:S(2)}) async-start(), calls=%async_computation.8 | async-start | bytes 1216512 | tf_op jit(solution)/shard_map/all_gather | solution.py:121
  9.4 244.8 %all-gather.14.cloned.1.call-start = ((), (), s32[]{:S(2)}) async-start(), calls=%async_computation.11 | async-start | bytes 1216512 | tf_op jit(solution)/shard_map/all_gather | solution.py:124
  10.0 361.4 %all-gather.18.cloned.1.call-start = ((), (), s32[]{:S(2)}) async-start(), calls=%async_computation.13 | async-start | bytes 1327104 | tf_op jit(solution)/shard_map/all_gather | solution.py:129
  10.6 360.9 %all-gather.16.cloned.1.call-start = ((), (), s32[]{:S(2)}) async-start(), calls=%async_computation.12 | async-start | bytes 7864320 | tf_op jit(solution)/shard_map/all_gather | solution.py:151
  55.2 124.3 %copy-start.27 = (f32[768]{0:T(1024)}, f32[768]{0:T(1024)S(1)}, u32[]{:S(2)}) copy-start(f32[768]{0:T(1024)S(1)} %convert_element_type.106) | copy-start | bytes 9220
  55.3 208.0 %copy-start.19 = (s32[1024]{0:T(1024)}, s32[1024]{0:T(1024)S(1)}, u32[]{:S(2)}) copy-start(s32[1024]{0:T(1024)S(1)} %fusion.95) | copy-start | bytes 12292
  55.3 204.3 %copy-start.21 = (f32[768]{0:T(1024)}, f32[768]{0:T(1024)S(1)}, u32[]{:S(2)}) copy-start(f32[768]{0:T(1024)S(1)} %convert_element_type.111) | copy-start | bytes 9220
  57.0 197.2 %copy-start.2 = (bf16[1,1024,768]{1,2,0:T(8,128)(2,1)}, bf16[1,1024,768]{1,2,0:T(8,128)(2,1)S(1)}, u32[]{:S(2)}) copy-start(bf16[1,1024,768]{1,2,0:T(8,128)(2,1)S(1)} %copy.42) | copy-start | bytes 4718596
  57.3 122.2 %copy-start.25 = (f32[1024]{0:T(1024)}, f32[1024]{0:T(1024)S(1)}, u32[]{:S(2)}) copy-start(f32[1024]{0:T(1024)S(1)} %broadcast_multiply_fusion.5) | copy-start | bytes 12292
  57.8 121.7 %copy-start.29 = (f32[1024]{0:T(1024)}, f32[1024]{0:T(1024)S(1)}, u32[]{:S(2)}) copy-start(f32[1024]{0:T(1024)S(1)} %add_rsqrt_fusion.1) | copy-start | bytes 12292
  254.2 5.0 copy-start.7
  254.2 5.0 copy-start.14
  260.9 1.7 copy-start.9
  262.5 143.8 %all-gather.20.cloned.1.call-start = ((), (), s32[]{:S(2)}) async-start(), calls=%async_computation.14 | async-start | bytes 1327104 | tf_op jit(solution)/shard_map/all_gather | solution.py:130
  263.3 106.5 %copy-start.4 = (bf16[1,1024,768]{1,2,0:T(8,128)(2,1)}, bf16[1,1024,768]{1,2,0:T(8,128)(2,1)S(1)}, u32[]{:S(2)}) copy-start(bf16[1,1024,768]{1,2,0:T(8,128)(2,1)S(1)} %copy.47) | copy-start | bytes 4718596
  263.3 106.5 %copy-start.15 = (f32[1024]{0:T(1024)}, f32[1024]{0:T(1024)S(1)}, u32[]{:S(2)}) copy-start(f32[1024]{0:T(1024)S(1)} %compare_convert_fusion.1) | copy-start | bytes 12292
  263.8 19.9 %collective-permute-start = (bf16[1024,768]{0,1:T(8,128)(2,1)S(1)}, bf16[1024,768]{0,1:T(8,128)(2,1)S(1)}, u32[]{:S(2)}, u32[]{:S(2)}) collective-permute-start(bf16[1024,768]{0,1:T(8,128)(2,1)S(1)} %fusion.87), channel_id=1, source_target_pairs={{0,1},{1,2},{2,3},{3,0},{4,5},{5,6},{6,7},{7,4},{8,9},{9,10},{10,1... | collective-permute-start | bytes 4718600 | tf_op jit(solution)/shard_map/ppermute | solution.py:178
  283.7 48.6 %collective-permute-start.1 = (bf16[1024,768]{0,1:T(8,128)(2,1)S(1)}, bf16[1024,768]{0,1:T(8,128)(2,1)}, u32[]{:S(2)}, u32[]{:S(2)}) collective-permute-start(bf16[1024,768]{0,1:T(8,128)(2,1)S(1)} %collective-permute-done), channel_id=1, source_target_pairs={{0,1},{1,2},{2,3},{3,0},{4,5},{5,6},{6,7},{7,4},{8,9},{9,10},{10,1... | collective-permute-start | bytes 4718600 | tf_op jit(solution)/shard_map/ppermute | solution.py:178
  332.3 21.9 %collective-permute-start.2 = (bf16[1024,768]{0,1:T(8,128)(2,1)}, bf16[1024,768]{0,1:T(8,128)(2,1)}, u32[]{:S(2)}, u32[]{:S(2)}) collective-permute-start(bf16[1024,768]{0,1:T(8,128)(2,1)} %collective-permute-done.1), channel_id=1, source_target_pairs={{0,1},{1,2},{2,3},{3,0},{4,5},{5,6},{6,7},{7,4},{8,9},{9,10},{10,1... | collective-permute-start | bytes 4718600 | tf_op jit(solution)/shard_map/ppermute | solution.py:178
  334.8 197.0 %reduce-scatter.11.cloned.1.call-start = ((), (), s32[]{:S(2)}) async-start(), calls=%async_computation.16 | async-start | bytes 15728640 | tf_op jit(solution)/shard_map/reduce_scatter | solution.py:186
  406.2 19.5 %copy-start.33 = (bf16[768,768]{1,0:T(8,128)(2,1)S(1)}, bf16[768,768]{1,0:T(8,128)(2,1)}, u32[]{:S(2)}) copy-start(bf16[768,768]{1,0:T(8,128)(2,1)} %all-gather.18.cloned.1.call-done) | copy-start | bytes 3538948
  423.1 2.6 copy-start.35
  433.6 199.9 %reduce-scatter.9.cloned.1.call-start = ((), (), s32[]{:S(2)}) async-start(), calls=%async_computation.15 | async-start | bytes 15728640 | tf_op jit(solution)/shard_map/reduce_scatter | solution.py:155
  447.8 445.2 %reduce-scatter.21.cloned.1.call-start = ((), (), s32[]{:S(2)}) async-start(), calls=%async_computation.21 | async-start | bytes 2654208 | tf_op jit(solution)/shard_map/reduce_scatter | solution.py:213
  459.2 72.6 %copy-start.18 = (f32[1024]{0:T(1024)S(1)}, f32[1024]{0:T(1024)}, u32[]{:S(2)}) copy-start(f32[1024]{0:T(1024)} %copy-done.17) | copy-start | bytes 12292
  459.2 72.6 %copy-start.22 = (f32[768]{0:T(1024)S(1)}, f32[768]{0:T(1024)}, u32[]{:S(2)}) copy-start(f32[768]{0:T(1024)} %copy-done.21) | copy-start | bytes 9220
  459.2 72.6 %copy-start.24 = (f32[1024]{0:T(1024)S(1)}, f32[1024]{0:T(1024)}, u32[]{:S(2)}) copy-start(f32[1024]{0:T(1024)} %copy-done.23) | copy-start | bytes 12292
  459.2 433.8 %reduce-scatter.23.cloned.1.call-start = ((), (), s32[]{:S(2)}) async-start(), calls=%async_computation.22 | async-start | bytes 2654208 | tf_op jit(solution)/shard_map/reduce_scatter | solution.py:214
  459.3 72.5 %copy-start.1 = (f32[1024,768]{0,1:T(8,128)S(1)}, f32[1024,768]{0,1:T(8,128)}, u32[]{:S(2)}) copy-start(f32[1024,768]{0,1:T(8,128)} %copy-done) | copy-start | bytes 9437188
  470.5 163.0 %copy-start.16 = (f32[1024]{0:T(1024)S(1)}, f32[1024]{0:T(1024)}, u32[]{:S(2)}) copy-start(f32[1024]{0:T(1024)} %copy-done.15) | copy-start | bytes 12292
  470.5 422.5 %reduce-scatter.19.cloned.1.call-start = ((), (), s32[]{:S(2)}) async-start(), calls=%async_computation.20 | async-start | bytes 2433024 | tf_op jit(solution)/shard_map/reduce_scatter | solution.py:220
  633.5 6.7 copy-start.13
  640.1 2.6 copy-start.5
  642.7 4.3 copy-start.6
  651.3 336.0 %reduce-scatter.13.cloned.1.call-start = ((), (), s32[]{:S(2)}) async-start(), calls=%async_computation.17 | async-start | bytes 2433024 | tf_op jit(solution)/shard_map/reduce_scatter | solution.py:217
  654.3 160.6 %copy-start.3 = (bf16[1,1024,768]{1,2,0:T(8,128)(2,1)S(1)}, bf16[1,1024,768]{1,2,0:T(8,128)(2,1)}, u32[]{:S(2)}) copy-start(bf16[1,1024,768]{1,2,0:T(8,128)(2,1)} %copy-done.2) | copy-start | bytes 4718596
  654.3 160.6 %copy-start.26 = (f32[1024]{0:T(1024)S(1)}, f32[1024]{0:T(1024)}, u32[]{:S(2)}) copy-start(f32[1024]{0:T(1024)} %copy-done.25) | copy-start | bytes 12292
  654.3 160.6 %copy-start.28 = (f32[768]{0:T(1024)S(1)}, f32[768]{0:T(1024)}, u32[]{:S(2)}) copy-start(f32[768]{0:T(1024)} %copy-done.27) | copy-start | bytes 9220
  654.3 160.6 %copy-start.30 = (f32[1024]{0:T(1024)S(1)}, f32[1024]{0:T(1024)}, u32[]{:S(2)}) copy-start(f32[1024]{0:T(1024)} %copy-done.29) | copy-start | bytes 12292
  814.9 9.4 copy-start.10
  819.8 271.2 %reduce-scatter.15.cloned.1.call-start = ((), (), s32[]{:S(2)}) async-start(), calls=%async_computation.18 | async-start | bytes 2433024 | tf_op jit(solution)/shard_map/reduce_scatter | solution.py:218
  824.3 371.5 %reduce-scatter.17.cloned.1.call-start = ((), (), s32[]{:S(2)}) async-start(), calls=%async_computation.19 | async-start | bytes 2433024 | tf_op jit(solution)/shard_map/reduce_scatter | solution.py:219
  824.3 3.0 copy-start.20
  830.2 3.6 copy-start.12
  830.2 3.6 copy-start.32
  833.9 1.7 copy-start.31
  (6 other events, 8.9 us)
Sparse Core Ops, SparseCore 0:
  10.9 56.7 all-gather.11
  70.6 52.9 all-gather.9
  126.5 52.9 all-gather.7
  182.3 52.9 all-gather.13
  237.3 39.9 all-gather.17
  279.3 60.4 all-gather.15
  341.9 41.0 all-gather.19
  433.7 97.9 reduce-scatter.10
  534.4 99.0 reduce-scatter.8
  637.4 68.9 reduce-scatter.20
  710.4 68.1 reduce-scatter.22
  784.3 98.1 reduce-scatter.18
  889.2 98.0 reduce-scatter.12
  993.0 97.9 reduce-scatter.14
  1097.6 98.0 reduce-scatter.16
